TPU v7x, 32 devices: a whole 2x2x4 slice. The times are simulated.
32 devices in a mesh: dp: 8 (over y, x, core), expert: 4 (over z).
Axes of the slice: x: 2, y: 2, z: 4, core: 2. Of those that a mesh axis runs over, the one named last changes fastest.
Arguments:
- tokens: bfloat16 [4096, 4096], P(('dp', 'expert')), may hold values from -6 to 6
- probs: bfloat16 [4096, 1], P(('dp', 'expert')), may hold values from 0.19921875 to 1
- routes: int32 [4096, 1], P(('dp', 'expert')), may hold values from 0 to 3; in each aligned block of 128 rows (0 to 127, 128 to 255, ...) at most 34 rows name the same one
- w_gate: bfloat16 [4, 4096, 1024], P('expert', 'dp'), may hold values from -0.09375 to 0.09375
- w_up: bfloat16 [4, 4096, 1024], P('expert', 'dp'), may hold values from -0.09375 to 0.09375
- w_down: bfloat16 [4, 1024, 4096], P('expert', None, 'dp'), may hold values from -0.1875 to 0.1875
- cotangent: bfloat16 [4096, 4096], P(('dp', 'expert')), may hold values from -6 to 6
Outputs:
- mixed: bfloat16 [4096, 4096], P(('dp', 'expert'))
- input_grad: bfloat16 [4096, 4096], P(('dp', 'expert'))
- grad_gate: bfloat16 [4, 4096, 1024], P('expert', 'dp')
- grad_up: bfloat16 [4, 4096, 1024], P('expert', 'dp')
- grad_down: bfloat16 [4, 1024, 4096], P('expert', None, 'dp')
Inputs may be any that keep to these rules, and one draw needn't show every extreme that they name: `routes`: each row names exactly one expert. Among the 128 rows of one device (aligned blocks), no expert is named more than 34 times, a bound that some block reaches.
All inputs are finite; a program needn't handle non-finite values.
Results may differ from a plain program's by a relative error of at most 0.025.
Values may be sent and summed in bfloat16 or wider, within the bound.
A program may use at most 128 MiB of HBM per device.

v0:
```python
import jax
import jax.numpy as jnp
from jax import lax
from jax.sharding import PartitionSpec as P


def slot_table(routes, experts_all, capacity):
    flat = routes.reshape(-1)
    hits = (flat[:, None] == jnp.arange(experts_all, dtype=jnp.int32)[None, :]).astype(jnp.int32)
    before = jnp.cumsum(hits, axis=0) - hits
    place = jnp.sum(before * hits, axis=1)
    target = flat * capacity + place
    table = jnp.arange(experts_all * capacity, dtype=jnp.int32)[:, None] == target[None, :]
    return table.astype(jnp.bfloat16)


def spread_rows(table, values, slices):
    shaped = values.reshape(values.shape[0], slices, values.shape[1] // slices)
    return jnp.einsum("st,tnk->nsk", table, shaped, preferred_element_type=jnp.float32).astype(
        jnp.bfloat16
    )


def to_rows(received, local_count):
    sources, slots, width = received.shape
    shaped = received.reshape(sources, local_count, slots // local_count, width)
    shaped = jnp.swapaxes(shaped, 1, 2)
    return shaped.reshape(sources * (slots // local_count), local_count, width)


def to_sources(rowwise, capacity):
    total, local_count, width = rowwise.shape
    shaped = rowwise.reshape(total // capacity, capacity, local_count, width)
    shaped = jnp.swapaxes(shaped, 1, 2)
    return shaped.reshape(total // capacity, local_count * capacity, width)


def collect(table, back, tok_rows, top):
    picked = jnp.einsum("st,nsk->tnk", table, back, preferred_element_type=jnp.float32)
    return picked.reshape(tok_rows, top, -1)


def per_device(tokens, probs, routes, w_gate, w_up, w_down, cotangent):
    local_count = w_gate.shape[0]
    n_dp = lax.axis_size("dp")
    n_exp = lax.axis_size("expert")
    experts_all = local_count * n_exp
    tok_rows, width = tokens.shape
    top = routes.shape[1]
    capacity = max(2, 17 * tok_rows * top // (16 * experts_all))
    blocks = n_dp * n_exp
    slot_width = width // n_dp
    table = slot_table(routes, experts_all, capacity)
    x_send = spread_rows(table, jnp.repeat(tokens, top, axis=0), n_dp)
    x_send = x_send.reshape(blocks, local_count * capacity, slot_width)
    weight = probs.astype(jnp.float32)
    scaled = (jnp.repeat(cotangent, top, axis=0).astype(jnp.float32) * weight).astype(jnp.bfloat16)
    x_got = lax.all_to_all(x_send, ("dp", "expert"), split_axis=0, concat_axis=0, tiled=True)
    rows = to_rows(x_got, local_count)
    part = rows
    gate = jnp.einsum("red,edf->ref", part, w_gate, preferred_element_type=jnp.float32)
    upper = jnp.einsum("red,edf->ref", part, w_up, preferred_element_type=jnp.float32)
    summed = lax.psum_scatter(
        jnp.stack([gate, upper], axis=2).astype(jnp.bfloat16), "dp", scatter_dimension=0, tiled=True
    ).astype(jnp.float32)
    gate_pre = summed[:, :, 0]
    up_value = summed[:, :, 1]
    sig = jax.nn.sigmoid(gate_pre)
    act = (gate_pre * sig * up_value).astype(jnp.bfloat16)
    act_all = lax.all_gather(act, "dp", axis=0, tiled=True)
    result = jnp.einsum("ref,efd->red", act_all, w_down, preferred_element_type=jnp.float32).astype(
        jnp.bfloat16
    )
    outgoing = to_sources(result, capacity)
    back = lax.all_to_all(outgoing, ("dp", "expert"), split_axis=0, concat_axis=0, tiled=True)
    back = back.reshape(n_dp, experts_all * capacity, slot_width)
    picked = collect(table, back, tok_rows, top)
    mixed = jnp.sum(picked * weight[..., None], axis=1).astype(jnp.bfloat16)
    dy_send = spread_rows(table, scaled, n_dp).reshape(blocks, local_count * capacity, slot_width)
    dy_got = lax.all_to_all(dy_send, ("dp", "expert"), split_axis=0, concat_axis=0, tiled=True)
    dout = to_rows(dy_got, local_count)
    grad_down = jnp.einsum("ref,red->efd", act_all, dout, preferred_element_type=jnp.float32)
    part = dout
    dact = lax.psum_scatter(
        jnp.einsum("red,efd->ref", part, w_down, preferred_element_type=jnp.float32).astype(
            jnp.bfloat16
        ),
        "dp",
        scatter_dimension=0,
        tiled=True,
    ).astype(jnp.float32)
    dgate = (dact * up_value * sig * (1.0 + gate_pre * (1.0 - sig))).astype(jnp.bfloat16)
    dup = (dact * gate_pre * sig).astype(jnp.bfloat16)
    dgate_all, dup_all = (
        lax.all_gather(dgate, "dp", axis=0, tiled=True),
        lax.all_gather(dup, "dp", axis=0, tiled=True),
    )
    grad_gate = jnp.einsum("red,ref->edf", rows, dgate_all, preferred_element_type=jnp.float32)
    grad_up = jnp.einsum("red,ref->edf", rows, dup_all, preferred_element_type=jnp.float32)
    slot_grad = jnp.einsum(
        "ref,edf->red", dgate_all, w_gate, preferred_element_type=jnp.float32
    ) + jnp.einsum("ref,edf->red", dup_all, w_up, preferred_element_type=jnp.float32)
    slot_grad = slot_grad.astype(jnp.bfloat16)
    returned = lax.all_to_all(
        to_sources(slot_grad, capacity), ("dp", "expert"), split_axis=0, concat_axis=0, tiled=True
    )
    returned = returned.reshape(n_dp, experts_all * capacity, slot_width)
    input_grad = jnp.sum(collect(table, returned, tok_rows, top), axis=1).astype(jnp.bfloat16)
    return (
        mixed,
        input_grad,
        grad_gate.astype(jnp.bfloat16),
        grad_up.astype(jnp.bfloat16),
        grad_down.astype(jnp.bfloat16),
    )


def solution(mesh):
    return jax.shard_map(
        per_device,
        mesh=mesh,
        in_specs=(
            P(("dp", "expert"), None),
            P(("dp", "expert"), None),
            P(("dp", "expert"), None),
            P("expert", "dp", None),
            P("expert", "dp", None),
            P("expert", None, "dp"),
            P(("dp", "expert"), None),
        ),
        out_specs=(
            P(("dp", "expert"), None),
            P(("dp", "expert"), None),
            P("expert", "dp", None),
            P("expert", "dp", None),
            P("expert", None, "dp"),
        ),
        check_vma=False,
    )
```

profile of v0, /device:TPU:1, one launch (start us, length us, event | category | flops | bytes accessed | tf_op | source)
XLA Modules:
  0.0 326.0 jit_solution(5524149168156521085)
XLA Ops:
  7.2 0.8 fusion.55
  8.0 0.2 reduce_window_sum.11
  8.2 0.8 select_reduce_fusion
  9.1 0.7 multiply_add_fusion
  9.7 1.7 fusion.26
  11.4 0.3 reshape.232
  11.7 39.8 %all_to_all.20 = bf16[32,34,512]{2,1,0:T(8,128)(2,1)} all-to-all(bf16[32,34,512]{2,1,0:T(8,128)(2,1)S(1)} %reshape.232), channel_id=1, replica_groups=mesh['dp'=8,'expert'=4] {'dp','expert'}, dimensions={0} | all-to-all | bytes 2228224 | tf_op jit(solution)/shard_map/all_to_all | solution.py:58
  51.5 1.5 reshape.233
  53.0 1.3 fusion.1
  54.4 0.3 copy-done.8
  54.7 1.3 fusion.2
  56.0 0.4 pad_maximum_fusion
  56.4 9.6 %copy.22 = bf16[1088,1,2,1024]{3,2,1,0:T(2,128)(2,1)S(1)} copy(bf16[1088,1,2,1024]{3,0,2,1:T(8,128)(2,1)S(1)} %pad_maximum_fusion) | data formatting | bytes 8912896
  66.0 3.9 %copy.28 = bf16[136,8,2,1024]{3,1,2,0:T(8,128)(2,1)} copy(bf16[136,8,2,1024]{3,2,1,0:T(2,128)(2,1)S(1)} %bitcast.140) | data formatting | bytes 8912896
  69.9 0.6 copy-done.12
  70.5 0.6 copy-done.5
  71.1 0.3 multiply_convert_fusion
  71.4 0.4 fusion.27
  71.8 0.3 reshape.240
  72.2 35.4 %all_to_all.21 = bf16[32,34,512]{2,1,0:T(8,128)(2,1)} all-to-all(bf16[32,34,512]{2,1,0:T(8,128)(2,1)S(1)} %reshape.240), channel_id=1, replica_groups=mesh['dp'=8,'expert'=4] {'dp','expert'}, dimensions={0} | all-to-all | bytes 2228224 | tf_op jit(solution)/shard_map/all_to_all | solution.py:80
  107.6 1.5 reshape.241
  109.0 2.8 fusion.3
  111.9 11.7 %reduce-scatter.7.cloned.1.call-done = bf16[136,2048]{1,0:T(8,128)(2,1)} async-done(((bf16[1088,2048]{1,0:T(8,128)(2,1)}), bf16[136,2048]{1,0:T(8,128)(2,1)}) %reduce-scatter.7.cloned.1.call-update) | async-done | bytes 557072
  123.6 2.3 reshape.249
  125.9 0.1 copy_convert_fusion
  126.0 42.7 %reduce-scatter.5.cloned.1.call-done = bf16[136,1,1024]{2,0,1:T(8,128)(2,1)} async-done(((bf16[1088,1,1024]{2,0,1:T(8,128)(2,1)}), bf16[136,1,1024]{2,0,1:T(8,128)(2,1)}) %reduce-scatter.5.cloned.1.call-update) | async-done | bytes 278544 | tf_op jit(solution)/shard_map/reduce_scatter | solution.py:84
  168.8 2.2 fusion.51
  171.0 0.5 all-gather.8.cloned.1.call-update
  171.6 0.2 all-gather.4.cloned.1.call-start
  171.8 0.4 all-gather.4.cloned.1.call-update
  172.2 28.0 %all-gather.6.cloned.1.call-done = bf16[1088,1,1024]{2,0,1:T(8,128)(2,1)} async-done(((bf16[136,1,1024]{2,0,1:T(8,128)(2,1)}), bf16[1088,1,1024]{2,0,1:T(8,128)(2,1)}) %all-gather.6.cloned.1.call-update) | async-done | bytes 2228240 | tf_op jit(solution)/shard_map/all_gather | solution.py:95
  200.1 4.4 %fusion.12 = f32[1088,512]{1,0:T(8,128)} fusion(bf16[1088,1,1024]{2,0,1:T(8,128)(2,1)} %all-gather.6.cloned.1.call-done, bf16[1,512,1024]{2,1,0:T(8,128)(2,1)S(1)} %copy-done), kind=kOutput, calls=%fused_computation.20 | convolution fusion | flops 1140850688 | bytes 5505024 | tf_op jit(solution)/shard_map/ref,edf->red/dot_general | solution.py:100
  204.6 26.3 %all-gather.8.cloned.1.call-done = bf16[1088,1,1024]{2,0,1:T(8,128)(2,1)} async-done(((bf16[136,1,1024]{2,0,1:T(8,128)(2,1)}), bf16[1088,1,1024]{2,0,1:T(8,128)(2,1)}) %all-gather.8.cloned.1.call-update) | async-done | bytes 2228240 | tf_op jit(solution)/shard_map/all_gather | solution.py:96
  230.8 3.7 %fusion.6 = bf16[1088,1,512]{2,0,1:T(8,128)(2,1)S(1)} fusion(f32[1088,512]{1,0:T(8,128)} %fusion.12, bf16[1088,1,1024]{2,0,1:T(8,128)(2,1)} %all-gather.8.cloned.1.call-done, bf16[1,512,1024]{2,1,0:T(8,128)(2,1)S(1)} %copy-done.9), kind=kOutput, calls=%fused_computation.14 | convolution fusion | flops 1141964800 | bytes 6619136 | tf_op jit(solution)/shard_map/ref,edf->red/dot_general | solution.py:102
  234.5 1.3 reshape_transpose_reshape.9
  235.8 4.6 %all-to-all-start.3 = ((bf16[32,34,512]{2,1,0:T(8,128)(2,1)}), bf16[32,34,512]{2,1,0:T(8,128)(2,1)S(1)}, u32[]{:S(2)}, u32[]{:S(2)}) async-start(bf16[32,34,512]{2,1,0:T(8,128)(2,1)} %reshape_transpose_reshape.9), calls=%async_computation.4 | async-start | bytes 2621440 | tf_op jit(solution)/shard_map/all_to_all | solution.py:104
  240.5 33.1 %all-gather.4.cloned.1.call-done = bf16[1088,1,1024]{2,0,1:T(8,128)(2,1)} async-done(((bf16[136,1,1024]{2,0,1:T(8,128)(2,1)}), bf16[1088,1,1024]{2,0,1:T(8,128)(2,1)}) %all-gather.4.cloned.1.call-update) | async-done | bytes 2228240 | tf_op jit(solution)/shard_map/all_gather | solution.py:70
  273.6 4.0 %fusion.5 = bf16[1088,1,512]{2,0,1:T(8,128)(2,1)} fusion(bf16[1088,1,1024]{2,0,1:T(8,128)(2,1)} %all-gather.4.cloned.1.call-done, bf16[1,1024,512]{2,1,0:T(8,128)(2,1)S(1)} %copy-done.11), kind=kOutput, calls=%fused_computation.13 | convolution fusion | flops 1141407744 | bytes 4390912 | tf_op jit(solution)/shard_map/ref,efd->red/dot_general | solution.py:71
  277.6 2.4 reshape_transpose_reshape.8
  279.9 4.5 %all-to-all-start.1 = ((bf16[32,34,512]{2,1,0:T(8,128)(2,1)}), bf16[32,34,512]{2,1,0:T(8,128)(2,1)}, u32[]{:S(2)}, u32[]{:S(2)}) async-start(bf16[32,34,512]{2,1,0:T(8,128)(2,1)} %reshape_transpose_reshape.8), calls=%async_computation.1 | async-start | bytes 2621440 | tf_op jit(solution)/shard_map/all_to_all | solution.py:75
  284.5 4.3 %fusion.28 = bf16[1,512,1024]{2,1,0:T(8,128)(2,1)} fusion(bf16[1088,512]{1,0:T(8,128)(2,1)S(1)} %copy-done.2, bf16[1088,1,1024]{2,0,1:T(8,128)(2,1)} %all-gather.8.cloned.1.call-done), kind=kOutput, calls=%fused_computation.33 | convolution fusion | flops 1141374976 | bytes 4390912 | tf_op jit(solution)/shard_map/red,ref->edf/dot_general | solution.py:99
  288.8 2.5 fusion.31
  291.3 2.5 fusion.34
  293.9 0.3 reshape.244
  294.3 1.5 convolution_convert_fusion
  295.8 20.6 %all-to-all-done.1 = bf16[32,34,512]{2,1,0:T(8,128)(2,1)} async-done(((bf16[32,34,512]{2,1,0:T(8,128)(2,1)}), bf16[32,34,512]{2,1,0:T(8,128)(2,1)}, u32[]{:S(2)}, u32[]{:S(2)}) %all-to-all-start.1) | async-done | bytes 1114144 | tf_op jit(solution)/shard_map/all_to_all | solution.py:75
  316.4 1.5 reshape.238
  318.0 1.5 fusion
  (34 shorter events, 0.5 us)
Async XLA Ops:
  7.2 45.8 %copy-start = (bf16[1,512,1024]{2,1,0:T(8,128)(2,1)S(1)}, bf16[1,512,1024]{2,1,0:T(8,128)(2,1)}, u32[]{:S(2)}) copy-start(bf16[1,512,1024]{2,1,0:T(8,128)(2,1)} %param.10) | copy-start | bytes 3145732
  7.2 116.4 %reduce-scatter.7.cloned.1.call-start = ((), (), s32[]{:S(2)}) async-start(), calls=%async_computation.10 | async-start | bytes 5013504
  53.0 1.4 copy-start.1
  53.0 1.6 copy-start.8
  69.9 0.7 copy-start.12
  69.9 1.2 copy-start.5
  69.9 98.9 %reduce-scatter.5.cloned.1.call-start = ((), (), s32[]{:S(2)}) async-start(), calls=%async_computation.7 | async-start | bytes 2506752 | tf_op jit(solution)/shard_map/reduce_scatter | solution.py:84
  72.2 36.9 %copy-start.10 = (bf16[1,1024,512]{2,1,0:T(8,128)(2,1)S(1)}, bf16[1,1024,512]{2,1,0:T(8,128)(2,1)}, u32[]{:S(2)}) copy-start(bf16[1,1024,512]{2,1,0:T(8,128)(2,1)} %param.12) | copy-start | bytes 3145732
  109.0 2.8 copy-start.3
  111.8 88.3 %all-gather.6.cloned.1.call-start = ((), (), s32[]{:S(2)}) async-start(), calls=%async_computation.8 | async-start | bytes 2506752 | tf_op jit(solution)/shard_map/all_gather | solution.py:95
  171.0 59.8 %all-gather.8.cloned.1.call-start = ((), (), s32[]{:S(2)}) async-start(), calls=%async_computation.9 | async-start | bytes 2506752 | tf_op jit(solution)/shard_map/all_gather | solution.py:96
  171.6 102.0 %all-gather.4.cloned.1.call-start = ((), (), s32[]{:S(2)}) async-start(), calls=%async_computation.6 | async-start | bytes 2506752 | tf_op jit(solution)/shard_map/all_gather | solution.py:70
  172.1 58.7 %copy-start.9 = (bf16[1,512,1024]{2,1,0:T(8,128)(2,1)S(1)}, bf16[1,512,1024]{2,1,0:T(8,128)(2,1)}, u32[]{:S(2)}) copy-start(bf16[1,512,1024]{2,1,0:T(8,128)(2,1)} %param.11) | copy-start | bytes 3145732
  234.5 39.1 %copy-start.11 = (bf16[1,1024,512]{2,1,0:T(8,128)(2,1)S(1)}, bf16[1,1024,512]{2,1,0:T(8,128)(2,1)}, u32[]{:S(2)}) copy-start(bf16[1,1024,512]{2,1,0:T(8,128)(2,1)} %param.12) | copy-start | bytes 3145732
  235.8 44.1 %all-to-all-start.3 = ((bf16[32,34,512]{2,1,0:T(8,128)(2,1)}), bf16[32,34,512]{2,1,0:T(8,128)(2,1)S(1)}, u32[]{:S(2)}, u32[]{:S(2)}) async-start(bf16[32,34,512]{2,1,0:T(8,128)(2,1)} %reshape_transpose_reshape.9), calls=%async_computation.4 | async-start | bytes 2621440 | tf_op jit(solution)/shard_map/all_to_all | solution.py:104
  277.6 6.9 %copy-start.2 = (bf16[1088,512]{1,0:T(8,128)(2,1)S(1)}, bf16[1088,512]{1,0:T(8,128)(2,1)}, u32[]{:S(2)}) copy-start(bf16[1088,512]{1,0:T(8,128)(2,1)} %copy-done.1) | copy-start | bytes 3342340
  279.9 36.5 %all-to-all-start.1 = ((bf16[32,34,512]{2,1,0:T(8,128)(2,1)}), bf16[32,34,512]{2,1,0:T(8,128)(2,1)}, u32[]{:S(2)}, u32[]{:S(2)}) async-start(bf16[32,34,512]{2,1,0:T(8,128)(2,1)} %reshape_transpose_reshape.8), calls=%async_computation.1 | async-start | bytes 2621440 | tf_op jit(solution)/shard_map/all_to_all | solution.py:75
  284.5 4.3 %copy-start.6 = (bf16[1088,1,1024]{2,0,1:T(8,128)(2,1)S(1)}, bf16[1088,1,1024]{2,0,1:T(8,128)(2,1)}, u32[]{:S(2)}) copy-start(bf16[1088,1,1024]{2,0,1:T(8,128)(2,1)} %all-gather.6.cloned.1.call-done) | copy-start | bytes 6684676
  288.8 2.5 copy-start.4
  288.8 2.5 copy-start.7
Sparse Core Ops, SparseCore 0:
  70.0 53.5 reduce-scatter.6
  126.9 41.7 reduce-scatter.4
  171.2 28.8 all-gather.5
  202.5 28.3 all-gather.7
  233.1 40.3 all-gather.3
where the time goes:
time: 327 us; the launch traced here: 326 us
  waiting for transfers between devices  163 us (50%)
  blocking collectives  75.2 us (23%)
  matrix products  32 us (10%)
  local copies, waits for them, and re-layouts  26.5 us (8%)
  between operations  14.1 us (4%)
  starting transfers between devices  9.55 us (3%)
  other arithmetic  5.48 us (2%)
    reduce_scatter x1, waiting for transfers between devices, per_device(): lax.psum_scatter(jnp.einsum('red,efd->ref', part, w_down, preferred_eleme...  42.7 us
    all_to_all x1, blocking collectives, per_device(): lax.all_to_all(x_send, ('dp', 'expert'), split_axis=0, concat_axis=0, til...  39.8 us
    all_to_all x1, blocking collectives, per_device(): lax.all_to_all(dy_send, ('dp', 'expert'), split_axis=0, concat_axis=0, ti...  35.4 us
    all_gather x1, waiting for transfers between devices, per_device(): act_all = lax.all_gather(act, 'dp', axis=0, tiled=True)  33.1 us
    all_gather x1, waiting for transfers between devices, per_device(): lax.all_gather(dgate, 'dp', axis=0, tiled=True)  28 us
    all_gather x1, waiting for transfers between devices, per_device(): lax.all_gather(dup, 'dp', axis=0, tiled=True)  26.3 us
    all_to_all x1, waiting for transfers between devices, per_device(): lax.all_to_all(outgoing, ('dp', 'expert'), split_axis=0, concat_axis=0, t...  20.6 us
    unnamed x29, local copies, waits for them, and re-layouts  17.2 us
  transfers between devices with their start and end apart: 7, of which 6 were waited for; matrix products, arithmetic and copies ran while one was open for 11% of the time, Pallas kernels for 0%

commit v1 on v0

--- a/solution.py
+++ b/solution.py
@@ -67,7 +67,13 @@
     up_value = summed[:, :, 1]
     sig = jax.nn.sigmoid(gate_pre)
     act = (gate_pre * sig * up_value).astype(jnp.bfloat16)
-    act_all = lax.all_gather(act, "dp", axis=0, tiled=True)
+    n_dev = lax.axis_size("dp")
+    current, shards = (act, [act])
+    for _ in range(n_dev - 1):
+        current = lax.ppermute(current, "dp", [(i, (i + 1) % n_dev) for i in range(n_dev)])
+        shards.insert(0, current)
+    ravelled = jnp.concatenate(shards, axis=0)
+    act_all = jnp.roll(ravelled, (lax.axis_index("dp") + 1) * act.shape[0], axis=0)
     result = jnp.einsum("ref,efd->red", act_all, w_down, preferred_element_type=jnp.float32).astype(
         jnp.bfloat16
     )

time: 327 us -> 312 us (0.954)
  waiting for transfers between devices: 163 us -> 126 us
  starting transfers between devices: 9.55 us -> 29.9 us
  local copies, waits for them, and re-layouts: 26.5 us -> 30.7 us
    all_gather x1 -> x0, waiting for transfers between devices: 33.1 us -> none  [per_device(): act_all = lax.all_gather(act, 'dp', axis=0, tiled=True)]
    ppermute x0 -> x7, waiting for transfers between devices: none -> 31.4 us  [per_device(): lax.ppermute(current, 'dp', [(i, (i + 1) % n_dev) for i in range(n_dev)])]
    all_gather x1, waiting for transfers between devices: 28 us -> 0.02 us  [per_device(): lax.all_gather(dgate, 'dp', axis=0, tiled=True)]
    all_to_all x1, waiting for transfers between devices: 0.01 us -> 18.1 us  [per_device(): lax.all_to_all(to_sources(slot_grad, capacity), ('dp', 'expert'), split_a...]
    ppermute x0 -> x7, starting transfers between devices: none -> 16.8 us  [per_device(): lax.ppermute(current, 'dp', [(i, (i + 1) % n_dev) for i in range(n_dev)])]
    all_to_all x1, waiting for transfers between devices: 20.6 us -> 5.69 us  [per_device(): lax.all_to_all(outgoing, ('dp', 'expert'), split_axis=0, concat_axis=0, t...]
    all_gather x1, waiting for transfers between devices: 26.3 us -> 16.6 us  [per_device(): lax.all_gather(dup, 'dp', axis=0, tiled=True)]
    all_to_all x1, starting transfers between devices: 4.54 us -> 9.75 us  [per_device(): lax.all_to_all(outgoing, ('dp', 'expert'), split_axis=0, concat_axis=0, t...]
  transfers between devices with their start and end apart: 7 -> 13, of which waited for: 6 -> 12; matrix products, arithmetic and copies ran while one was open for 11% -> 11% of each run, Pallas kernels for 0% -> 0%
where the time goes in v1:
time: 312 us
  waiting for transfers between devices  126 us (40%)
  blocking collectives  75.2 us (24%)
  local copies, waits for them, and re-layouts  30.7 us (10%)
  starting transfers between devices  29.9 us (10%)
  matrix products  29.9 us (10%)
  between operations  14.2 us (5%)
  other arithmetic  5.37 us (2%)
    reduce_scatter x1, waiting for transfers between devices, per_device(): lax.psum_scatter(jnp.einsum('red,efd->ref', part, w_down, preferred_eleme...  42.7 us
    all_to_all x1, blocking collectives, per_device(): lax.all_to_all(x_send, ('dp', 'expert'), split_axis=0, concat_axis=0, til...  39.8 us
    all_to_all x1, blocking collectives, per_device(): lax.all_to_all(dy_send, ('dp', 'expert'), split_axis=0, concat_axis=0, ti...  35.4 us
    ppermute x7, waiting for transfers between devices, per_device(): lax.ppermute(current, 'dp', [(i, (i + 1) % n_dev) for i in range(n_dev)])  31.4 us
    unnamed x44, local copies, waits for them, and re-layouts  19.5 us
    all_to_all x1, waiting for transfers between devices, per_device(): lax.all_to_all(to_sources(slot_grad, capacity), ('dp', 'expert'), split_a...  18.1 us
    ppermute x7, starting transfers between devices, per_device(): lax.ppermute(current, 'dp', [(i, (i + 1) % n_dev) for i in range(n_dev)])  16.8 us
    all_gather x1, waiting for transfers between devices, per_device(): lax.all_gather(dup, 'dp', axis=0, tiled=True)  16.6 us
  transfers between devices with their start and end apart: 13, of which 12 were waited for; matrix products, arithmetic and copies ran while one was open for 11% of the time, Pallas kernels for 0%

profile of v1, /device:TPU:1, one launch (start us, length us, event | category | flops | bytes accessed | tf_op | source)
XLA Modules:
  0.0 311.5 jit_solution(10330194249298606505)
XLA Ops:
  9.7 1.7 fusion.28
  11.8 39.8 %all_to_all.20 = bf16[32,34,512]{2,1,0:T(8,128)(2,1)} all-to-all(bf16[32,34,512]{2,1,0:T(8,128)(2,1)S(1)} %reshape.232), channel_id=1, replica_groups=mesh['dp'=8,'expert'=4] {'dp','expert'}, dimensions={0} | all-to-all | bytes 2228224 | tf_op jit(solution)/shard_map/all_to_all | solution.py:58
  51.6 1.5 reshape.233
  53.0 1.3 fusion.1
  54.7 1.3 fusion.2
  56.4 9.6 %copy.22 = bf16[1088,1,2,1024]{3,2,1,0:T(2,128)(2,1)S(1)} copy(bf16[1088,1,2,1024]{3,0,2,1:T(8,128)(2,1)S(1)} %pad_maximum_fusion) | data formatting | bytes 8912896
  66.0 3.9 %copy.28 = bf16[136,8,2,1024]{3,1,2,0:T(8,128)(2,1)} copy(bf16[136,8,2,1024]{3,2,1,0:T(2,128)(2,1)S(1)} %bitcast.140) | data formatting | bytes 8912896
  72.2 35.4 %all_to_all.21 = bf16[32,34,512]{2,1,0:T(8,128)(2,1)} all-to-all(bf16[32,34,512]{2,1,0:T(8,128)(2,1)S(1)} %reshape.240), channel_id=1, replica_groups=mesh['dp'=8,'expert'=4] {'dp','expert'}, dimensions={0} | all-to-all | bytes 2228224 | tf_op jit(solution)/shard_map/all_to_all | solution.py:86
  107.6 1.5 reshape.241
  109.1 2.8 fusion.3
  111.9 11.7 %reduce-scatter.7.cloned.1.call-done = bf16[136,2048]{1,0:T(8,128)(2,1)} async-done(((bf16[1088,2048]{1,0:T(8,128)(2,1)}), bf16[136,2048]{1,0:T(8,128)(2,1)}) %reduce-scatter.7.cloned.1.call-update) | async-done | bytes 557072
  123.6 2.3 reshape.249
  126.0 42.7 %reduce-scatter.5.cloned.1.call-done = bf16[136,1,1024]{2,0,1:T(8,128)(2,1)} async-done(((bf16[1088,1,1024]{2,0,1:T(8,128)(2,1)}), bf16[136,1,1024]{2,0,1:T(8,128)(2,1)}) %reduce-scatter.5.cloned.1.call-update) | async-done | bytes 278544 | tf_op jit(solution)/shard_map/reduce_scatter | solution.py:90
  168.8 2.1 fusion.53
  170.9 2.0 collective-permute-start
  172.9 3.5 %collective-permute-done = bf16[136,1,1024]{2,0,1:T(8,128)(2,1)S(1)} collective-permute-done((bf16[136,1,1024]{2,0,1:T(8,128)(2,1)S(1)}, bf16[136,1,1024]{2,0,1:T(8,128)(2,1)S(1)}, u32[]{:S(2)}, u32[]{:S(2)}) %collective-permute-start) | collective-permute-done | bytes 278560 | tf_op jit(solution)/shard_map/ppermute | solution.py:73
  176.4 2.5 collective-permute-start.1
  178.9 6.5 %collective-permute-done.1 = bf16[136,1,1024]{2,0,1:T(8,128)(2,1)S(1)} collective-permute-done((bf16[136,1,1024]{2,0,1:T(8,128)(2,1)S(1)}, bf16[136,1,1024]{2,0,1:T(8,128)(2,1)S(1)}, u32[]{:S(2)}, u32[]{:S(2)}) %collective-permute-start.1) | collective-permute-done | bytes 278560 | tf_op jit(solution)/shard_map/ppermute | solution.py:73
  185.4 2.5 collective-permute-start.2
  187.8 3.5 %collective-permute-done.2 = bf16[136,1,1024]{2,0,1:T(8,128)(2,1)S(1)} collective-permute-done((bf16[136,1,1024]{2,0,1:T(8,128)(2,1)S(1)}, bf16[136,1,1024]{2,0,1:T(8,128)(2,1)S(1)}, u32[]{:S(2)}, u32[]{:S(2)}) %collective-permute-start.2) | collective-permute-done | bytes 278560 | tf_op jit(solution)/shard_map/ppermute | solution.py:73
  191.3 2.5 collective-permute-start.3
  193.8 7.0 %collective-permute-done.3 = bf16[136,1,1024]{2,0,1:T(8,128)(2,1)S(1)} collective-permute-done((bf16[136,1,1024]{2,0,1:T(8,128)(2,1)S(1)}, bf16[136,1,1024]{2,0,1:T(8,128)(2,1)S(1)}, u32[]{:S(2)}, u32[]{:S(2)}) %collective-permute-start.3) | collective-permute-done | bytes 278560 | tf_op jit(solution)/shard_map/ppermute | solution.py:73
  200.8 2.5 collective-permute-start.4
  203.3 3.5 %collective-permute-done.4 = bf16[136,1,1024]{2,0,1:T(8,128)(2,1)S(1)} collective-permute-done((bf16[136,1,1024]{2,0,1:T(8,128)(2,1)S(1)}, bf16[136,1,1024]{2,0,1:T(8,128)(2,1)S(1)}, u32[]{:S(2)}, u32[]{:S(2)}) %collective-permute-start.4) | collective-permute-done | bytes 278560 | tf_op jit(solution)/shard_map/ppermute | solution.py:73
  206.8 2.5 collective-permute-start.5
  209.3 3.5 %collective-permute-done.5 = bf16[136,1,1024]{2,0,1:T(8,128)(2,1)S(1)} collective-permute-done((bf16[136,1,1024]{2,0,1:T(8,128)(2,1)S(1)}, bf16[136,1,1024]{2,0,1:T(8,128)(2,1)S(1)}, u32[]{:S(2)}, u32[]{:S(2)}) %collective-permute-start.5) | collective-permute-done | bytes 278560 | tf_op jit(solution)/shard_map/ppermute | solution.py:73
  212.8 2.5 collective-permute-start.6
  215.3 3.9 %collective-permute-done.6 = bf16[136,1,1024]{2,0,1:T(8,128)(2,1)S(1)} collective-permute-done((bf16[136,1,1024]{2,0,1:T(8,128)(2,1)S(1)}, bf16[136,1,1024]{2,0,1:T(8,128)(2,1)S(1)}, u32[]{:S(2)}, u32[]{:S(2)}) %collective-permute-start.6) | collective-permute-done | bytes 278560 | tf_op jit(solution)/shard_map/ppermute | solution.py:73
  219.6 2.0 copy-done.6
  221.7 1.3 fusion.5
  223.0 1.3 reshape_transpose_reshape.8
  224.3 9.8 %all-to-all-start.1 = ((bf16[32,34,512]{2,1,0:T(8,128)(2,1)}), bf16[32,34,512]{2,1,0:T(8,128)(2,1)S(1)}, u32[]{:S(2)}, u32[]{:S(2)}) async-start(bf16[32,34,512]{2,1,0:T(8,128)(2,1)} %reshape_transpose_reshape.8), calls=%async_computation.1 | async-start | bytes 2621440 | tf_op jit(solution)/shard_map/all_to_all | solution.py:81
  234.1 4.4 %fusion.12 = f32[1088,512]{1,0:T(8,128)} fusion(bf16[1088,1,1024]{2,0,1:T(8,128)(2,1)} %all-gather.3.cloned.1.call-done, bf16[1,512,1024]{2,1,0:T(8,128)(2,1)S(1)} %copy-done.10), kind=kOutput, calls=%fused_computation.20 | convolution fusion | flops 1140850688 | bytes 5505024 | tf_op jit(solution)/shard_map/ref,edf->red/dot_general | solution.py:106
  238.5 16.6 %all-gather.5.cloned.1.call-done = bf16[1088,1,1024]{2,0,1:T(8,128)(2,1)} async-done(((bf16[136,1,1024]{2,0,1:T(8,128)(2,1)}), bf16[1088,1,1024]{2,0,1:T(8,128)(2,1)}) %all-gather.5.cloned.1.call-update) | async-done | bytes 2228240 | tf_op jit(solution)/shard_map/all_gather | solution.py:102
  255.0 4.0 %fusion.6 = bf16[1088,1,512]{2,0,1:T(8,128)(2,1)S(1)} fusion(f32[1088,512]{1,0:T(8,128)} %fusion.12, bf16[1088,1,1024]{2,0,1:T(8,128)(2,1)} %all-gather.5.cloned.1.call-done, bf16[1,512,1024]{2,1,0:T(8,128)(2,1)} %param.11), kind=kOutput, calls=%fused_computation.14 | convolution fusion | flops 1141964800 | bytes 6619136 | tf_op jit(solution)/shard_map/ref,edf->red/dot_general | solution.py:108
  259.0 1.2 reshape_transpose_reshape.9
  260.2 5.7 %all-to-all-done.1 = bf16[32,34,512]{2,1,0:T(8,128)(2,1)S(1)} async-done(((bf16[32,34,512]{2,1,0:T(8,128)(2,1)}), bf16[32,34,512]{2,1,0:T(8,128)(2,1)S(1)}, u32[]{:S(2)}, u32[]{:S(2)}) %all-to-all-start.1) | async-done | bytes 1114144 | tf_op jit(solution)/shard_map/all_to_all | solution.py:81
  265.9 3.2 %all-to-all-start.3 = ((bf16[32,34,512]{2,1,0:T(8,128)(2,1)}), bf16[32,34,512]{2,1,0:T(8,128)(2,1)S(1)}, u32[]{:S(2)}, u32[]{:S(2)}) async-start(bf16[32,34,512]{2,1,0:T(8,128)(2,1)} %reshape_transpose_reshape.9), calls=%async_computation.4 | async-start | bytes 2621440 | tf_op jit(solution)/shard_map/all_to_all | solution.py:110
  269.1 4.6 %fusion.36 = bf16[1,1024,512]{2,1,0:T(8,128)(2,1)} fusion(bf16[1088,512]{1,0:T(8,128)(2,1)} %copy-done.4, bf16[2176,1,1024]{2,0,1:T(8,128)(2,1)} %copy-done.6, s32[]{:T(128)S(6)} %select_n.14), kind=kOutput, calls=%fused_computation.37 | convolution fusion | flops 1141374976 | bytes 4390916 | tf_op jit(solution)/shard_map/ref,red->efd/dot_general | solution.py:88
  273.7 2.5 fusion.30
  276.2 2.5 fusion.33
  278.7 1.2 reshape.238
  279.9 1.4 copy.26
  281.3 1.5 fusion
  282.8 18.1 %all-to-all-done.3 = bf16[32,34,512]{2,1,0:T(8,128)(2,1)S(1)} async-done(((bf16[32,34,512]{2,1,0:T(8,128)(2,1)}), bf16[32,34,512]{2,1,0:T(8,128)(2,1)S(1)}, u32[]{:S(2)}, u32[]{:S(2)}) %all-to-all-start.3) | async-done | bytes 1114144 | tf_op jit(solution)/shard_map/all_to_all | solution.py:110
  300.9 1.2 reshape.244
  302.1 1.4 copy.27
  303.5 1.5 convolution_convert_fusion
  (61 shorter events, 6.5 us)
Async XLA Ops:
  7.2 101.9 %copy-start = (bf16[1,1024,512]{2,1,0:T(8,128)(2,1)S(1)}, bf16[1,1024,512]{2,1,0:T(8,128)(2,1)}, u32[]{:S(2)}) copy-start(bf16[1,1024,512]{2,1,0:T(8,128)(2,1)} %param.12) | copy-start | bytes 3145732
  7.2 116.4 %reduce-scatter.7.cloned.1.call-start = ((), (), s32[]{:S(2)}) async-start(), calls=%async_computation.9 | async-start | bytes 5013504
  11.7 41.3 %copy-start.9 = (bf16[1,512,1024]{2,1,0:T(8,128)(2,1)S(1)}, bf16[1,512,1024]{2,1,0:T(8,128)(2,1)}, u32[]{:S(2)}) copy-start(bf16[1,512,1024]{2,1,0:T(8,128)(2,1)} %param.10) | copy-start | bytes 3145732
  53.0 1.4 copy-start.2
  53.0 1.6 copy-start.11
  69.9 0.7 copy-start.12
  69.9 1.2 copy-start.5
  69.9 98.9 %reduce-scatter.5.cloned.1.call-start = ((), (), s32[]{:S(2)}) async-start(), calls=%async_computation.6 | async-start | bytes 2506752 | tf_op jit(solution)/shard_map/reduce_scatter | solution.py:90
  109.0 2.8 copy-start.4
  111.8 122.2 %all-gather.3.cloned.1.call-start = ((), (), s32[]{:S(2)}) async-start(), calls=%async_computation.7 | async-start | bytes 2506752 | tf_op jit(solution)/shard_map/all_gather | solution.py:101
  170.9 84.1 %all-gather.5.cloned.1.call-start = ((), (), s32[]{:S(2)}) async-start(), calls=%async_computation.8 | async-start | bytes 2506752 | tf_op jit(solution)/shard_map/all_gather | solution.py:102
  170.9 5.5 %collective-permute-start = (bf16[136,1,1024]{2,0,1:T(8,128)(2,1)S(1)}, bf16[136,1,1024]{2,0,1:T(8,128)(2,1)S(1)}, u32[]{:S(2)}, u32[]{:S(2)}) collective-permute-start(bf16[136,1,1024]{2,0,1:T(8,128)(2,1)S(1)} %get-tuple-element.7), channel_id=1, source_target_pairs={{0,4},{4,8},{8,12},{12,16},{16,20},{20,24},{24,28},{28,0},{1,5},{5... | collective-permute-start | bytes 835592 | tf_op jit(solution)/shard_map/ppermute | solution.py:73
  176.4 9.0 %collective-permute-start.1 = (bf16[136,1,1024]{2,0,1:T(8,128)(2,1)S(1)}, bf16[136,1,1024]{2,0,1:T(8,128)(2,1)S(1)}, u32[]{:S(2)}, u32[]{:S(2)}) collective-permute-start(bf16[136,1,1024]{2,0,1:T(8,128)(2,1)S(1)} %collective-permute-done), channel_id=1, source_target_pairs={{0,4},{4,8},{8,12},{12,16},{16,20},{20,24},{24,28},{28,0},{1,5},{5... | collective-permute-start | bytes 835592 | tf_op jit(solution)/shard_map/ppermute | solution.py:73
  185.4 6.0 %collective-permute-start.2 = (bf16[136,1,1024]{2,0,1:T(8,128)(2,1)S(1)}, bf16[136,1,1024]{2,0,1:T(8,128)(2,1)S(1)}, u32[]{:S(2)}, u32[]{:S(2)}) collective-permute-start(bf16[136,1,1024]{2,0,1:T(8,128)(2,1)S(1)} %collective-permute-done.1), channel_id=1, source_target_pairs={{0,4},{4,8},{8,12},{12,16},{16,20},{20,24},{24,28},{28,0},{1,5},{5... | collective-permute-start | bytes 835592 | tf_op jit(solution)/shard_map/ppermute | solution.py:73
  191.3 9.5 %collective-permute-start.3 = (bf16[136,1,1024]{2,0,1:T(8,128)(2,1)S(1)}, bf16[136,1,1024]{2,0,1:T(8,128)(2,1)S(1)}, u32[]{:S(2)}, u32[]{:S(2)}) collective-permute-start(bf16[136,1,1024]{2,0,1:T(8,128)(2,1)S(1)} %collective-permute-done.2), channel_id=1, source_target_pairs={{0,4},{4,8},{8,12},{12,16},{16,20},{20,24},{24,28},{28,0},{1,5},{5... | collective-permute-start | bytes 835592 | tf_op jit(solution)/shard_map/ppermute | solution.py:73
  200.8 6.0 %collective-permute-start.4 = (bf16[136,1,1024]{2,0,1:T(8,128)(2,1)S(1)}, bf16[136,1,1024]{2,0,1:T(8,128)(2,1)S(1)}, u32[]{:S(2)}, u32[]{:S(2)}) collective-permute-start(bf16[136,1,1024]{2,0,1:T(8,128)(2,1)S(1)} %collective-permute-done.3), channel_id=1, source_target_pairs={{0,4},{4,8},{8,12},{12,16},{16,20},{20,24},{24,28},{28,0},{1,5},{5... | collective-permute-start | bytes 835592 | tf_op jit(solution)/shard_map/ppermute | solution.py:73
  206.8 6.0 %collective-permute-start.5 = (bf16[136,1,1024]{2,0,1:T(8,128)(2,1)S(1)}, bf16[136,1,1024]{2,0,1:T(8,128)(2,1)S(1)}, u32[]{:S(2)}, u32[]{:S(2)}) collective-permute-start(bf16[136,1,1024]{2,0,1:T(8,128)(2,1)S(1)} %collective-permute-done.4), channel_id=1, source_target_pairs={{0,4},{4,8},{8,12},{12,16},{16,20},{20,24},{24,28},{28,0},{1,5},{5... | collective-permute-start | bytes 835592 | tf_op jit(solution)/shard_map/ppermute | solution.py:73
  212.8 6.4 %collective-permute-start.6 = (bf16[136,1,1024]{2,0,1:T(8,128)(2,1)S(1)}, bf16[136,1,1024]{2,0,1:T(8,128)(2,1)S(1)}, u32[]{:S(2)}, u32[]{:S(2)}) collective-permute-start(bf16[136,1,1024]{2,0,1:T(8,128)(2,1)S(1)} %collective-permute-done.5), channel_id=1, source_target_pairs={{0,4},{4,8},{8,12},{12,16},{16,20},{20,24},{24,28},{28,0},{1,5},{5... | collective-permute-start | bytes 835592 | tf_op jit(solution)/shard_map/ppermute | solution.py:73
  219.6 2.1 copy-start.6
  223.0 11.1 %copy-start.10 = (bf16[1,512,1024]{2,1,0:T(8,128)(2,1)S(1)}, bf16[1,512,1024]{2,1,0:T(8,128)(2,1)}, u32[]{:S(2)}) copy-start(bf16[1,512,1024]{2,1,0:T(8,128)(2,1)} %param.10) | copy-start | bytes 3145732
  224.3 41.6 %all-to-all-start.1 = ((bf16[32,34,512]{2,1,0:T(8,128)(2,1)}), bf16[32,34,512]{2,1,0:T(8,128)(2,1)S(1)}, u32[]{:S(2)}, u32[]{:S(2)}) async-start(bf16[32,34,512]{2,1,0:T(8,128)(2,1)} %reshape_transpose_reshape.8), calls=%async_computation.1 | async-start | bytes 2621440 | tf_op jit(solution)/shard_map/all_to_all | solution.py:81
  265.9 35.0 %all-to-all-start.3 = ((bf16[32,34,512]{2,1,0:T(8,128)(2,1)}), bf16[32,34,512]{2,1,0:T(8,128)(2,1)S(1)}, u32[]{:S(2)}, u32[]{:S(2)}) async-start(bf16[32,34,512]{2,1,0:T(8,128)(2,1)} %reshape_transpose_reshape.9), calls=%async_computation.4 | async-start | bytes 2621440 | tf_op jit(solution)/shard_map/all_to_all | solution.py:110
  269.1 4.6 %copy-start.3 = (bf16[1088,512]{1,0:T(8,128)(2,1)S(1)}, bf16[1088,512]{1,0:T(8,128)(2,1)}, u32[]{:S(2)}) copy-start(bf16[1088,512]{1,0:T(8,128)(2,1)} %copy-done.2) | copy-start | bytes 3342340
  269.1 4.6 %copy-start.8 = (bf16[1088,1,1024]{2,0,1:T(8,128)(2,1)S(1)}, bf16[1088,1,1024]{2,0,1:T(8,128)(2,1)}, u32[]{:S(2)}) copy-start(bf16[1088,1,1024]{2,0,1:T(8,128)(2,1)} %all-gather.5.cloned.1.call-done) | copy-start | bytes 6684676
  273.7 2.5 copy-start.7
  300.9 4.1 %copy-start.1 = (bf16[1,1024,512]{2,1,0:T(8,128)(2,1)S(1)}, bf16[1,1024,512]{2,1,0:T(8,128)(2,1)}, u32[]{:S(2)}) copy-start(bf16[1,1024,512]{2,1,0:T(8,128)(2,1)} %param.12) | copy-start | bytes 3145732
Sparse Core Ops, SparseCore 0:
  70.0 53.5 reduce-scatter.6
  127.0 41.7 reduce-scatter.4
  171.3 32.4 all-gather.2
  215.4 39.5 all-gather.4
